TPU v7x, 512 devices: a whole 4x4x16 slice. The times are simulated.
512 devices in a mesh: grid: 64 (over y_lo, z, core), dp: 8 (over y_hi, x).
Axes of the slice: x: 4, y: 4 (y_hi: 2, y_lo: 2; y = y_hi * 2 + y_lo), z: 16, core: 2. Of those that a mesh axis runs over, the one named last changes fastest.
Arguments:
- field: bfloat16 [65536, 1024], P('grid', 'dp'), may hold values from -6 to 6
- cotangent: bfloat16 [65536, 1024], P('grid', 'dp'), may hold values from -6 to 6
- mode_blocks: int32 [8], replicated, may hold values from 0 to 4095, as said below
- spectral: bfloat16 [2, 64, 64, 64], P(None, 'grid'), may hold values from -6 to 6
- w_in: bfloat16 [64, 256], replicated, may hold values from -0.75 to 0.75
- b_in: float32 [256], replicated, may hold values from -3 to 3
- w_out: bfloat16 [256, 64], replicated, may hold values from -0.375 to 0.375
- b_out: float32 [64], replicated, may hold values from -3 to 3
Outputs:
- output: bfloat16 [65536, 1024], P('grid', 'dp')
- field_grad: bfloat16 [65536, 1024], P('grid', 'dp')
- spectral_grad: float32 [2, 64, 64, 64], P(None, 'grid')
- w_in_grad: float32 [64, 256], replicated
- b_in_grad: float32 [256], replicated
- w_out_grad: float32 [256, 64], replicated
- b_out_grad: float32 [64], replicated
Inputs may be any that keep to these rules, and one draw needn't show every extreme that they name: `mode_blocks`: distinct block numbers; 0 and 4095 are always among them.
All inputs are finite; a program needn't handle non-finite values.
Results may differ from a plain program's by a relative error of at most 0.013.
Values may be sent and summed in bfloat16 or wider, within the bound.
No kernel may reach another device: no remote copies, remote signals or barrier semaphores. Data moves between devices by JAX's collectives and lax.ppermute only.
A program may use at most 64 MiB of HBM per device.

v0:
```python
import math
import jax
import jax.numpy as jnp
from jax import lax
from jax.sharding import PartitionSpec as P

NX = 65536
BLK = 8


def mode_list(mode_blocks, block_width):
    offsets = jnp.arange(block_width, dtype=jnp.int32)
    return (mode_blocks[:, None] * block_width + offsets[None, :]).reshape(-1)


def forward_table(modes, first_row, count, length):
    rows_here = first_row + jnp.arange(count, dtype=jnp.int32)
    product = modes[:, None] * rows_here[None, :] % length
    phase = product.astype(jnp.float32) * (2.0 * math.pi / length)
    scale = 1.0 / math.sqrt(length)
    table = jnp.stack([jnp.cos(phase) * scale, -jnp.sin(phase) * scale], axis=1)
    return table.reshape(2 * modes.shape[0], count).astype(jnp.bfloat16)


def inverse_table(forward):
    return (forward.astype(jnp.float32) * 2.0).astype(jnp.bfloat16).T


def gelu_grad(pre):
    _, pull = jax.vjp(jax.nn.gelu, pre)
    return pull(jnp.ones_like(pre))[0]


def mix(real, imag, weight_re, weight_im):
    best = lax.Precision.HIGHEST
    out_re = jnp.einsum("kbi,kio->kbo", real, weight_re, precision=best) - jnp.einsum(
        "kbi,kio->kbo", imag, weight_im, precision=best
    )
    out_im = jnp.einsum("kbi,kio->kbo", real, weight_im, precision=best) + jnp.einsum(
        "kbi,kio->kbo", imag, weight_re, precision=best
    )
    return (out_re, out_im)


def mix_grads(real, imag, grad_re, grad_im, weight_re, weight_im):
    best = lax.Precision.HIGHEST
    w_re = jnp.einsum("kbi,kbo->kio", real, grad_re, precision=best) + jnp.einsum(
        "kbi,kbo->kio", imag, grad_im, precision=best
    )
    w_im = jnp.einsum("kbi,kbo->kio", real, grad_im, precision=best) - jnp.einsum(
        "kbi,kbo->kio", imag, grad_re, precision=best
    )
    in_re = jnp.einsum("kbo,kio->kbi", grad_re, weight_re, precision=best) + jnp.einsum(
        "kbo,kio->kbi", grad_im, weight_im, precision=best
    )
    in_im = jnp.einsum("kbo,kio->kbi", grad_im, weight_re, precision=best) - jnp.einsum(
        "kbo,kio->kbi", grad_re, weight_im, precision=best
    )
    return (w_re, w_im, in_re, in_im)


def pointwise_pass(field, spec, cotangent, w_in, b_in, w_out, b_out):
    chans = w_in.shape[0]
    shape = field.shape
    spec_rows = spec.reshape(-1, chans)
    pre = jnp.dot(spec_rows, w_in, preferred_element_type=jnp.float32) + b_in
    hidden = jax.nn.gelu(pre).astype(jnp.bfloat16)
    out = jnp.dot(hidden, w_out, preferred_element_type=jnp.float32) + b_out
    result = (
        (field.reshape(-1, chans).astype(jnp.float32) + out).astype(jnp.bfloat16).reshape(shape)
    )
    upstream = cotangent.reshape(-1, chans)
    grad_w_out = jnp.einsum("nh,nc->hc", hidden, upstream, preferred_element_type=jnp.float32)
    grad_b_out = jnp.sum(upstream.astype(jnp.float32), axis=0)
    grad_hidden = jnp.einsum("nc,hc->nh", upstream, w_out, preferred_element_type=jnp.float32)
    grad_pre = (grad_hidden * gelu_grad(pre)).astype(jnp.bfloat16)
    grad_w_in = jnp.einsum("nc,nh->ch", spec_rows, grad_pre, preferred_element_type=jnp.float32)
    grad_b_in = jnp.sum(grad_pre.astype(jnp.float32), axis=0)
    grad_spec = (
        jnp.einsum("nh,ch->nc", grad_pre, w_in, preferred_element_type=jnp.float32)
        .astype(jnp.bfloat16)
        .reshape(shape)
    )
    return (result, grad_spec, (grad_w_in, grad_b_in, grad_w_out, grad_b_out))


def local(field, cotangent, mode_blocks, spectral, w_in, b_in, w_out, b_out):
    rows = field.shape[0]
    width = field.shape[1]
    chans = w_in.shape[0]
    ncol = width // chans
    own = spectral.shape[1]
    modes = mode_list(mode_blocks, BLK)
    columns_total = ncol * lax.axis_size("dp")
    first = lax.axis_index("grid") * rows
    forward_here = forward_table(modes, first, rows, NX)
    inverse_here = inverse_table(forward_here)
    weight_re = spectral[0].astype(jnp.float32)
    weight_im = spectral[1].astype(jnp.float32)
    part = forward_here
    modal = lax.psum_scatter(
        jnp.dot(part, field, preferred_element_type=jnp.float32).reshape(
            own * lax.axis_size("grid"), 2 * width
        ),
        "grid",
        scatter_dimension=0,
        tiled=True,
    ).reshape(own, 2, ncol, chans)
    real = modal[:, 0]
    imag = modal[:, 1]
    out_re, out_im = mix(real, imag, weight_re, weight_im)
    mixed = jnp.stack([out_re, out_im], axis=1).reshape(own, 2 * width).astype(jnp.bfloat16)
    piece = lax.all_gather(mixed, "grid", axis=0, tiled=True)
    count = piece.shape[0]
    part = inverse_here
    spec = jnp.dot(
        part, piece.reshape(2 * count, width), preferred_element_type=jnp.float32
    ).astype(jnp.bfloat16)
    output, grad_spec, sums = pointwise_pass(field, spec, cotangent, w_in, b_in, w_out, b_out)
    part = inverse_here
    grad_modal = lax.psum_scatter(
        jnp.einsum("rm,rw->mw", part, grad_spec, preferred_element_type=jnp.float32).reshape(
            own * lax.axis_size("grid"), 2 * width
        ),
        "grid",
        scatter_dimension=0,
        tiled=True,
    ).reshape(own, 2, ncol, chans)
    w_re, w_im, in_re, in_im = mix_grads(
        real, imag, grad_modal[:, 0], grad_modal[:, 1], weight_re, weight_im
    )
    grad_in = jnp.stack([in_re, in_im], axis=1).reshape(own, 2 * width).astype(jnp.bfloat16)
    piece = lax.all_gather(grad_in, "grid", axis=0, tiled=True)
    count = piece.shape[0]
    part = forward_here
    back = jnp.einsum(
        "mr,mw->rw", part, piece.reshape(2 * count, width), preferred_element_type=jnp.float32
    )
    field_grad = (cotangent.astype(jnp.float32) + back).astype(jnp.bfloat16)
    spectral_part = jnp.stack([w_re, w_im], axis=0)
    spectral_sum = lax.psum(spectral_part.astype(jnp.bfloat16), "dp").astype(jnp.float32)
    grad_w_in, grad_b_in, grad_w_out, grad_b_out = lax.psum(
        (sums[0], sums[1], sums[2], sums[3]), ("grid", "dp")
    )
    inv_cols = 1.0 / columns_total
    return (
        output,
        field_grad,
        spectral_sum * inv_cols,
        grad_w_in * inv_cols,
        grad_b_in * inv_cols,
        grad_w_out * inv_cols,
        grad_b_out * inv_cols,
    )


def solution(mesh):
    in_specs = (
        P("grid", "dp"),
        P("grid", "dp"),
        P(),
        P(None, "grid", None, None),
        P(),
        P(),
        P(),
        P(),
    )
    out_specs = (P("grid", "dp"), P("grid", "dp"), P(None, "grid", None, None), P(), P(), P(), P())
    return jax.shard_map(local, mesh=mesh, in_specs=in_specs, out_specs=out_specs, check_vma=False)
```

profile of v0, /device:TPU:1, one launch (start us, length us, event | category | flops | bytes accessed | tf_op | source)
XLA Modules:
  0.0 1456.2 jit_solution(12951280648803934894)
XLA Ops:
  7.3 0.7 broadcast_multiply_fusion.4
  8.1 1.2 cosine_multiply_fusion
  10.0 0.6 reshape.368
  12.2 1.3 dynamic-slice
  13.5 363.8 %all-reduce.8.cloned.1.call-done = f32[64,256]{1,0:T(8,128)} async-done(((f32[64,256]{1,0:T(8,128)}), f32[64,256]{1,0:T(8,128)}) %all-reduce.8.cloned.1.call-update) | async-done | bytes 65552
  377.3 1.4 dynamic-slice_reduce_fusion.1
  379.4 61.0 %all-gather = bf16[64,1,256]{2,1,0:T(2,128)(2,1)S(1)} all-gather(bf16[1,1,256]{2,1,0:T(2,128)(2,1)S(1)} %reshape.385), channel_id=1, replica_groups=mesh['grid'=64,'dp'=8] {'grid'}, dimensions={0}, use_global_device_ids=true | all-gather | bytes 33280 | tf_op jit(solution)/shard_map/all_gather | solution.py:113
  441.1 0.9 multiply_convert_fusion
  442.0 1.5 convert_reduce_fusion
  443.5 0.9 fusion.49
  444.9 0.9 fusion.50
  446.6 101.6 %all-reduce.2 = (f32[256]{0:T(256)S(1)}, f32[64]{0:T(128)S(1)}) all-reduce(f32[256]{0:T(256)S(1)} %get-tuple-element.17, f32[64]{0:T(128)S(1)} %convert_reduce_fusion.1), channel_id=1, replica_groups=mesh['grid'=64,'dp'=8] {'grid','dp'}, use_global_device_ids=true, to_apply=%region_5.6 | all-reduce | flops 320 | bytes 2560 | tf_op jit(solution)/shard_map/psum | solution.py:142
  548.2 0.6 broadcast_multiply_fusion.2
  549.8 0.6 reshape.379
  550.7 1.0 reshape.376
  551.7 437.2 %all-reduce.12.cloned.1.call-done = (f32[64,256]{1,0:T(8,128)}, f32[256,64]{0,1:T(8,128)}) async-done(((f32[64,256]{1,0:T(8,128)}, f32[256,64]{0,1:T(8,128)}), (f32[64,256]{1,0:T(8,128)}, f32[256,64]{0,1:T(8,128)})) %all-reduce.12.cloned.1.call-update) | async-done | bytes 131088 | tf_op jit(solution)/shard_map/psum | solution.py:142
  988.9 1.5 broadcast_multiply_fusion
  990.4 1.5 broadcast_multiply_fusion.1
  991.9 351.2 %all-reduce.10.cloned.1.call-done = f32[64,256]{1,0:T(8,128)} async-done(((f32[64,256]{1,0:T(8,128)}), f32[64,256]{1,0:T(8,128)}) %all-reduce.10.cloned.1.call-update) | async-done | bytes 65552
  1343.1 1.4 dynamic-slice_reduce_fusion
  1345.8 34.1 %psum.35 = bf16[2,1,64,64]{3,2,1,0:T(8,128)(2,1)S(1)} all-reduce(bf16[2,1,64,64]{3,2,1,0:T(8,128)(2,1)S(1)} %pad_maximum_fusion), channel_id=1, replica_groups=mesh['grid'=64,'dp'=8] {'dp'}, use_global_device_ids=true, to_apply=%region_2.3 | all-reduce | flops 8192 | bytes 32768 | tf_op jit(solution)/shard_map/psum | solution.py:141
  1380.0 0.6 convert_multiply_fusion
  1381.0 67.5 %all-gather.1 = bf16[64,1,256]{2,1,0:T(2,128)(2,1)S(1)} all-gather(bf16[1,1,256]{2,1,0:T(2,128)(2,1)S(1)} %reshape.387), channel_id=1, replica_groups=mesh['grid'=64,'dp'=8] {'grid'}, dimensions={0}, use_global_device_ids=true | all-gather | bytes 33280 | tf_op jit(solution)/shard_map/all_gather | solution.py:133
  1448.7 1.0 fusion.9
  (65 shorter events, 8.2 us)
Async XLA Ops:
  7.2 433.9 %copy-start = (bf16[64,256]{1,0:T(8,128)(2,1)S(1)}, bf16[64,256]{1,0:T(8,128)(2,1)}, u32[]{:S(2)}) copy-start(bf16[64,256]{1,0:T(8,128)(2,1)} %param.12) | copy-start | bytes 98308
  7.2 2.6 copy-start.2
  7.2 3.6 copy-start.1
  7.2 370.1 %all-reduce.8.cloned.1.call-start = ((), (), s32[]{:S(2)}) async-start(), calls=%async_computation | async-start | bytes 131072
  10.7 978.2 %all-reduce.12.cloned.1.call-start = ((), (), s32[]{:S(2)}) async-start(), calls=%async_computation.2 | async-start | bytes 262144 | tf_op jit(solution)/shard_map/psum | solution.py:142
  11.3 367.4 %copy-start.3 = (bf16[2,1,64,64]{3,2,1,0:T(8,128)(2,1)S(1)}, bf16[2,1,64,64]{3,2,1,0:T(8,128)(2,1)}, u32[]{:S(2)}) copy-start(bf16[2,1,64,64]{3,2,1,0:T(8,128)(2,1)} %param.11) | copy-start | bytes 49156
  11.5 429.6 %copy-start.6 = (f32[256]{0:T(256)S(1)}, f32[256]{0:T(256)}, u32[]{:S(2)}) copy-start(f32[256]{0:T(256)} %param.13) | copy-start | bytes 3076
  441.1 0.9 copy-start.4
  444.9 104.0 %copy-start.5 = (f32[64]{0:T(128)S(1)}, f32[64]{0:T(128)}, u32[]{:S(2)}) copy-start(f32[64]{0:T(128)} %param.15) | copy-start | bytes 772
  548.8 794.3 %all-reduce.10.cloned.1.call-start = ((), (), s32[]{:S(2)}) async-start(), calls=%async_computation.1 | async-start | bytes 131072
Sparse Core Ops, SparseCore 0:
  11.5 365.7 all-reduce.7
  548.9 439.9 all-reduce.11
  992.4 350.6 all-reduce.9
where the time goes:
time: 1460 us
  waiting for transfers between devices  1150 us (79%)
  blocking collectives  264 us (18%)
    unnamed x5, waiting for transfers between devices  715 us
    psum x1, waiting for transfers between devices, local(): lax.psum((sums[0], sums[1], sums[2], sums[3]), ('grid', 'dp'))  437 us
    psum x1, blocking collectives, local(): lax.psum((sums[0], sums[1], sums[2], sums[3]), ('grid', 'dp'))  102 us
    all_gather x1, blocking collectives, local(): piece = lax.all_gather(grad_in, 'grid', axis=0, tiled=True)  67.5 us
    all_gather x1, blocking collectives, local(): piece = lax.all_gather(mixed, 'grid', axis=0, tiled=True)  61 us
    psum x1, blocking collectives, local(): lax.psum(spectral_part.astype(jnp.bfloat16), 'dp').astype(jnp.float32)  34.1 us
  transfers between devices with their start and end apart: 3, of which 3 were waited for; matrix products, arithmetic and copies ran while one was open for 1% of the time, Pallas kernels for 0%

commit v1 on v0

--- a/solution.py
+++ b/solution.py
@@ -140,7 +140,7 @@
     spectral_part = jnp.stack([w_re, w_im], axis=0)
     spectral_sum = lax.psum(spectral_part.astype(jnp.bfloat16), "dp").astype(jnp.float32)
     grad_w_in, grad_b_in, grad_w_out, grad_b_out = lax.psum(
-        (sums[0], sums[1], sums[2], sums[3]), ("grid", "dp")
+        lax.psum((sums[0], sums[1], sums[2], sums[3]), "grid"), "dp"
     )
     inv_cols = 1.0 / columns_total
     return (

time: 1460 us -> 1150 us (0.79)
  waiting for transfers between devices: 1150 us -> 818 us
  blocking collectives: 264 us -> 287 us
    psum x1, waiting for transfers between devices: 437 us -> 84.9 us  [local(): lax.psum(lax.psum((sums[0], sums[1], sums[2], sums[3]), 'grid'), 'dp')]
    psum x1 -> x2, blocking collectives: 102 us -> 124 us  [the longest x1 104 us: local(): lax.psum((sums[0], sums[1], sums[2], sums[3]), 'grid')]
    unnamed x5, waiting for transfers between devices: 715 us -> 733 us
  transfers between devices with their start and end apart: 3 -> 3, of which waited for: 3 -> 3; matrix products, arithmetic and copies ran while one was open for 1% -> 0% of each run, Pallas kernels for 0% -> 0%
where the time goes in v1:
time: 1150 us
  waiting for transfers between devices  818 us (71%)
  blocking collectives  287 us (25%)
  between operations  14.1 us (1%)
    unnamed x5, waiting for transfers between devices  733 us
    psum x1, blocking collectives, local(): lax.psum((sums[0], sums[1], sums[2], sums[3]), 'grid')  104 us
    psum x1, waiting for transfers between devices, local(): lax.psum(lax.psum((sums[0], sums[1], sums[2], sums[3]), 'grid'), 'dp')  84.9 us
    all_gather x1, blocking collectives, local(): piece = lax.all_gather(grad_in, 'grid', axis=0, tiled=True)  68.3 us
    all_gather x1, blocking collectives, local(): piece = lax.all_gather(mixed, 'grid', axis=0, tiled=True)  61 us
    psum x1, blocking collectives, local(): lax.psum(spectral_part.astype(jnp.bfloat16), 'dp').astype(jnp.float32)  34.5 us
  transfers between devices with their start and end apart: 3, of which 3 were waited for; matrix products, arithmetic and copies ran while one was open for 0% of the time, Pallas kernels for 0%

profile of v1, /device:TPU:1, one launch (start us, length us, event | category | flops | bytes accessed | tf_op | source)
XLA Modules:
  0.0 1148.8 jit_solution(15727350426920977653)
XLA Ops:
  8.1 1.2 cosine_multiply_fusion
  12.2 1.3 dynamic-slice
  13.6 363.7 %all-reduce.10.cloned.1.call-done = f32[64,256]{1,0:T(8,128)} async-done(((f32[64,256]{1,0:T(8,128)}), f32[64,256]{1,0:T(8,128)}) %all-reduce.10.cloned.1.call-update) | async-done | bytes 65552
  377.3 1.3 dynamic-slice_reduce_fusion.1
  379.4 61.0 %all-gather = bf16[64,1,256]{2,1,0:T(2,128)(2,1)S(1)} all-gather(bf16[1,1,256]{2,1,0:T(2,128)(2,1)S(1)} %reshape.385), channel_id=1, replica_groups=mesh['grid'=64,'dp'=8] {'grid'}, dimensions={0}, use_global_device_ids=true | all-gather | bytes 33280 | tf_op jit(solution)/shard_map/all_gather | solution.py:113
  441.1 0.9 multiply_convert_fusion
  441.9 1.5 convert_reduce_fusion
  443.4 0.9 fusion.49
  444.4 1.1 convolution_convert_fusion
  445.5 104.2 %all-reduce.2 = (f32[256]{0:T(256)S(1)}, f32[64]{0:T(128)S(1)}) all-reduce(f32[256]{0:T(256)S(1)} %get-tuple-element.22, f32[64]{0:T(128)S(1)} %convert_reduce_fusion.1), channel_id=1, replica_groups=mesh['grid'=64,'dp'=8] {'grid'}, use_global_device_ids=true, to_apply=%region_6.7 | all-reduce | flops 320 | bytes 2560 | tf_op jit(solution)/shard_map/psum | solution.py:143
  549.7 19.5 %all-reduce.4 = (f32[256]{0:T(256)S(1)}, f32[64]{0:T(128)S(1)}) all-reduce(f32[256]{0:T(256)S(1)} %get-tuple-element.7, f32[64]{0:T(128)S(1)} %get-tuple-element.8), channel_id=1, replica_groups=mesh['grid'=64,'dp'=8] {'dp'}, use_global_device_ids=true, to_apply=%region_7.8 | all-reduce | flops 320 | bytes 2560 | tf_op jit(solution)/shard_map/psum | solution.py:142
  569.8 1.2 copy.30
  571.0 1.0 reshape.378
  572.0 1.2 fusion.48
  573.8 0.9 fusion.50
  575.5 1.0 reshape.376
  577.0 369.6 %all-reduce.12.cloned.1.call-done = (f32[64,256]{1,0:T(8,128)}, f32[64,256]{1,0:T(8,128)}, f32[256,64]{0,1:T(8,128)}) async-done(((f32[64,256]{1,0:T(8,128)}, f32[64,256]{1,0:T(8,128)}, f32[256,64]{0,1:T(8,128)}), (f32[64,256]{1,0:T(8,128)}, f32[64,256]{1,0:T(8,128)}, f32[256,64]{0,1:T(8,128)})) %all-reduce.12.cloned.1.call-update) | async-done | bytes 196624
  946.7 1.3 dynamic-slice_reduce_fusion
  949.4 34.5 %psum.63 = bf16[2,1,64,64]{3,2,1,0:T(8,128)(2,1)S(1)} all-reduce(bf16[2,1,64,64]{3,2,1,0:T(8,128)(2,1)S(1)} %pad_maximum_fusion), channel_id=1, replica_groups=mesh['grid'=64,'dp'=8] {'dp'}, use_global_device_ids=true, to_apply=%region_2.3 | all-reduce | flops 8192 | bytes 32768 | tf_op jit(solution)/shard_map/psum | solution.py:141
  984.3 68.3 %all-gather.1 = bf16[64,1,256]{2,1,0:T(2,128)(2,1)S(1)} all-gather(bf16[1,1,256]{2,1,0:T(2,128)(2,1)S(1)} %reshape.387), channel_id=1, replica_groups=mesh['grid'=64,'dp'=8] {'grid'}, dimensions={0}, use_global_device_ids=true | all-gather | bytes 33280 | tf_op jit(solution)/shard_map/all_gather | solution.py:133
  1052.8 1.0 fusion.9
  1054.4 84.9 %all-reduce.14.cloned.1.call-done = (f32[64,256]{1,0:T(8,128)}, f32[256,64]{0,1:T(8,128)}) async-done(((f32[64,256]{1,0:T(8,128)}, f32[256,64]{0,1:T(8,128)}), (f32[64,256]{1,0:T(8,128)}, f32[256,64]{0,1:T(8,128)})) %all-reduce.14.cloned.1.call-update) | async-done | bytes 131088 | tf_op jit(solution)/shard_map/psum | solution.py:142
  1139.3 1.5 broadcast_multiply_fusion
  1140.8 1.5 broadcast_multiply_fusion.1
  (66 shorter events, 10.2 us)
Async XLA Ops:
  7.2 433.9 %copy-start = (bf16[64,256]{1,0:T(8,128)(2,1)S(1)}, bf16[64,256]{1,0:T(8,128)(2,1)}, u32[]{:S(2)}) copy-start(bf16[64,256]{1,0:T(8,128)(2,1)} %param.12) | copy-start | bytes 98308
  7.2 2.6 copy-start.2
  7.2 3.6 copy-start.1
  7.2 370.1 %all-reduce.10.cloned.1.call-start = ((), (), s32[]{:S(2)}) async-start(), calls=%async_computation | async-start | bytes 131072
  10.7 936.0 %all-reduce.12.cloned.1.call-start = ((), (), s32[]{:S(2)}) async-start(), calls=%async_computation.1 | async-start | bytes 393216
  11.3 367.4 %copy-start.3 = (bf16[2,1,64,64]{3,2,1,0:T(8,128)(2,1)S(1)}, bf16[2,1,64,64]{3,2,1,0:T(8,128)(2,1)}, u32[]{:S(2)}) copy-start(bf16[2,1,64,64]{3,2,1,0:T(8,128)(2,1)} %param.11) | copy-start | bytes 49156
  11.5 429.5 %copy-start.6 = (f32[256]{0:T(256)S(1)}, f32[256]{0:T(256)}, u32[]{:S(2)}) copy-start(f32[256]{0:T(256)} %param.13) | copy-start | bytes 3076
  441.1 0.9 copy-start.4
  445.5 129.2 %copy-start.5 = (f32[64]{0:T(128)S(1)}, f32[64]{0:T(128)}, u32[]{:S(2)}) copy-start(f32[64]{0:T(128)} %param.15) | copy-start | bytes 772
  576.5 562.9 %all-reduce.14.cloned.1.call-start = ((), (), s32[]{:S(2)}) async-start(), calls=%async_computation.2 | async-start | bytes 262144 | tf_op jit(solution)/shard_map/psum | solution.py:142
Sparse Core Ops, SparseCore 0:
  11.5 365.7 all-reduce.9
  576.6 370.0 all-reduce.11
  1053.9 85.3 all-reduce.13
